TPU v7x, 128 devices: a whole 4x4x4 slice. The times are simulated.
128 devices in a mesh: member: 2 (over y_hi), gridy: 8 (over x, core), gridx: 8 (over z, y_lo).
Axes of the slice: x: 4, y: 4 (y_hi: 2, y_lo: 2; y = y_hi * 2 + y_lo), z: 4, core: 2. Of those that a mesh axis runs over, the one named last changes fastest.
Arguments:
- temp: float32 [4, 4, 512, 2048], P('member', None, 'gridy', 'gridx'), may hold values from -6 to 6
- salt: float32 [4, 4, 512, 2048], P('member', None, 'gridy', 'gridx'), may hold values from -6 to 6
- uvel: float32 [4, 4, 512, 2048], P('member', None, 'gridy', 'gridx'), may hold values from -3 to 3
- vvel: float32 [4, 4, 512, 2048], P('member', None, 'gridy', 'gridx'), may hold values from -3 to 3
- eta: float32 [4, 512, 2048], P('member', 'gridy', 'gridx'), may hold values from -6 to 6
- land_mask: int32 [512, 2048], P('gridy', 'gridx'), may hold values 0 or 1
- clone_source: int32 [4], P('member'), may hold values from 0 to 3
Outputs:
- new_temp: float32 [4, 4, 512, 2048], P('member', None, 'gridy', 'gridx')
- new_salt: float32 [4, 4, 512, 2048], P('member', None, 'gridy', 'gridx')
- new_uvel: float32 [4, 4, 512, 2048], P('member', None, 'gridy', 'gridx')
- new_vvel: float32 [4, 4, 512, 2048], P('member', None, 'gridy', 'gridx')
- new_eta: float32 [4, 512, 2048], P('member', 'gridy', 'gridx')
- overturning: float32 [4, 4, 512], P('member', None, 'gridy')
- clone_weight: float32 [4], P('member')
All inputs are finite; a program needn't handle non-finite values. No bound on the sum of `land_mask` on one device may be relied on, other than what follows from the above.
Results may differ from a plain program's by a relative error of at most 0.0001.
Values sent between devices are 32-bit elements; how exact they have to be, the bound alone decides.
A program may use at most 128 MiB of HBM per device.

v0:
```python
import jax
import jax.numpy as jnp
from jax import lax
from jax.sharding import PartitionSpec as P

STEPS = 2
ITERS = 3
ALPHA_T = 0.8
BETA_S = 0.6
PRESS_K = 0.25
STEP_DT = 0.1
KAPPA = 0.1
VISCOSITY = 0.1
DRAG_K = 0.05
CORI_K = 1.0
SURF_C = 4.0
DIV_K = 0.5
GRAV_K = 0.5


def padded_2(block, sides, width):
    for axis, dim in sides:
        count = lax.axis_size(axis)
        forward = [(i, i + 1) for i in range(count - 1)]
        forward.append((count - 1, 0))
        backward = [(target, source) for source, target in forward]
        low = lax.ppermute(
            lax.slice_in_dim(block, block.shape[dim] - width, None, axis=dim), axis, forward
        )
        high = lax.ppermute(lax.slice_in_dim(block, 0, width, axis=dim), axis, backward)
        block = jnp.concatenate([low, block, high], axis=dim)
    return block


def pressure(temp, salt):
    return PRESS_K * jnp.cumsum(BETA_S * salt - ALPHA_T * temp, axis=-3)


def split_rims(padded, south_keep, north_keep):
    east_side = padded[..., 1:-1, 2:]
    west_side = padded[..., 1:-1, :-2]
    north_side = padded[..., 2:, 1:-1]
    south_side = padded[..., :-2, 1:-1]
    north_side = north_side.at[..., -1, :].multiply(north_keep)
    south_side = south_side.at[..., 0, :].multiply(south_keep)
    return (east_side, west_side, north_side, south_side)


def volume_sides(fields, south_keep, north_keep):
    padded = padded_2(jnp.stack(fields), (("gridy", 3), ("gridx", 4)), 1)
    return split_rims(padded, south_keep, north_keep)


def surface_sides(fields, south_keep, north_keep):
    padded = padded_2(jnp.stack(fields), (("gridy", 2), ("gridx", 3)), 1)
    return split_rims(padded, south_keep, north_keep)


def surface_apply(field, south_keep, north_keep):
    east_side, west_side, north_side, south_side = surface_sides((field,), south_keep, north_keep)
    return (1.0 + 4.0 * SURF_C) * field - SURF_C * (
        east_side[0] + west_side[0] + north_side[0] + south_side[0]
    )


def member_total(values):
    return jnp.sum(values, axis=(1, 2))


def squared_norm(residual):
    return lax.psum(member_total(residual * residual), ("gridy", "gridx"))


def widen(values):
    return values[:, None, None]


def surface_solve(rhs, south_keep, north_keep):
    solution = jnp.zeros_like(rhs)
    residual = rhs
    direction = rhs
    norm_now = squared_norm(residual)
    for count in range(ITERS):
        image = surface_apply(direction, south_keep, north_keep)
        alpha = norm_now / lax.psum(member_total(direction * image), ("gridy", "gridx"))
        solution = solution + widen(alpha) * direction
        residual = residual - widen(alpha) * image
        norm_next = squared_norm(residual)
        direction = residual + widen(norm_next / norm_now) * direction
        norm_now = norm_next
    return solution


def shards(temp, salt, uvel, vvel, eta, land_mask, clone_source):
    levels = temp.shape[1]
    rows = temp.shape[2]
    cols = temp.shape[3]
    ocean = land_mask.astype(jnp.float32)
    tile_row = lax.axis_index("gridy")
    tile_count = lax.axis_size("gridy")
    total_rows = rows * tile_count
    total_cols = cols * lax.axis_size("gridx")
    south_keep = (tile_row > 0).astype(jnp.float32)
    north_keep = (tile_row < tile_count - 1).astype(jnp.float32)
    latitude = (tile_row * rows + jnp.arange(rows, dtype=jnp.int32)).astype(jnp.float32) + 0.5
    coriolis = (CORI_K * (2.0 * latitude / total_rows - 1.0))[:, None]
    for count in range(STEPS):
        press = pressure(temp, salt)
        east_side, west_side, north_side, south_side = volume_sides(
            (temp, salt, uvel, vvel, press), south_keep, north_keep
        )
        lap_temp = east_side[0] + west_side[0] + north_side[0] + south_side[0] - 4.0 * temp
        lap_salt = east_side[1] + west_side[1] + north_side[1] + south_side[1] - 4.0 * salt
        lap_uvel = east_side[2] + west_side[2] + north_side[2] + south_side[2] - 4.0 * uvel
        lap_vvel = east_side[3] + west_side[3] + north_side[3] + south_side[3] - 4.0 * vvel
        temp_next = ocean * (
            temp
            - STEP_DT
            * 0.5
            * (uvel * (east_side[0] - west_side[0]) + vvel * (north_side[0] - south_side[0]))
            + KAPPA * lap_temp
        )
        salt_next = ocean * (
            salt
            - STEP_DT
            * 0.5
            * (uvel * (east_side[1] - west_side[1]) + vvel * (north_side[1] - south_side[1]))
            + KAPPA * lap_salt
        )
        ustar = ocean * (
            uvel
            + STEP_DT * (coriolis * vvel - 0.5 * (east_side[4] - west_side[4]) - DRAG_K * uvel)
            + VISCOSITY * lap_uvel
        )
        vstar = ocean * (
            vvel
            + STEP_DT * (-coriolis * uvel - 0.5 * (north_side[4] - south_side[4]) - DRAG_K * vvel)
            + VISCOSITY * lap_vvel
        )
        trans_u = jnp.sum(ustar, axis=1)
        trans_v = jnp.sum(vstar, axis=1)
        east_t, west_t, north_t, south_t = surface_sides((trans_u, trans_v), south_keep, north_keep)
        rhs = eta - DIV_K * 0.5 * (east_t[0] - west_t[0] + (north_t[1] - south_t[1]))
        eta = surface_solve(rhs, south_keep, north_keep)
        east_e, west_e, north_e, south_e = surface_sides((eta,), south_keep, north_keep)
        uvel = ocean * (ustar - GRAV_K * 0.5 * (east_e[0] - west_e[0])[:, None])
        vvel = ocean * (vstar - GRAV_K * 0.5 * (north_e[0] - south_e[0])[:, None])
        temp = temp_next
        salt = salt_next
    zonal_scale = 1.0 / jnp.sqrt(jnp.float32(total_cols))
    score_scale = 1.0 / jnp.sqrt(jnp.float32(levels * total_rows))
    lat_weight = latitude / total_rows
    zonal_local = jnp.sum(vvel, axis=3)
    zonal_whole = lax.psum(zonal_local, "gridx")
    overturn = jnp.cumsum(zonal_whole, axis=1) * zonal_scale
    score = lax.psum(jnp.sum(overturn * lat_weight, axis=(1, 2)) * score_scale, "gridy")
    state_stack = jnp.stack((temp, salt, uvel, vvel))
    every_state, every_eta, every_score = (
        lax.all_gather(state_stack, "member", axis=1, tiled=True),
        lax.all_gather(eta, "member", axis=0, tiled=True),
        lax.all_gather(score, "member", axis=0, tiled=True),
    )
    picked = jnp.take(every_state, clone_source, axis=1)
    new_eta = jnp.take(every_eta, clone_source, axis=0)
    clone_weight = jnp.take(every_score, clone_source, axis=0) - jnp.mean(every_score)
    return (picked[0], picked[1], picked[2], picked[3], new_eta, overturn, clone_weight)


def solution(mesh):
    in_specs = (
        P("member", None, "gridy", "gridx"),
        P("member", None, "gridy", "gridx"),
        P("member", None, "gridy", "gridx"),
        P("member", None, "gridy", "gridx"),
        P("member", "gridy", "gridx"),
        P("gridy", "gridx"),
        P("member"),
    )
    out_specs = (
        P("member", None, "gridy", "gridx"),
        P("member", None, "gridy", "gridx"),
        P("member", None, "gridy", "gridx"),
        P("member", None, "gridy", "gridx"),
        P("member", "gridy", "gridx"),
        P("member", None, "gridy"),
        P("member"),
    )
    return jax.shard_map(shards, mesh=mesh, in_specs=in_specs, out_specs=out_specs, check_vma=False)
```

profile of v0, /device:TPU:1, one launch (start us, length us, event | category | flops | bytes accessed | tf_op | source)
XLA Modules:
  0.0 1724.0 jit_solution(7264022242541431259)
XLA Ops:
  15.9 2.1 fusion.186
  18.0 1.9 copy.16
  21.2 1.9 copy.14
  23.1 3.5 collective-permute-start.2
  26.7 3.0 pad_maximum_fusion.5
  29.8 2.2 scatter-mul.81
  32.0 2.2 scatter-mul.80
  37.6 2.9 fusion.179
  40.7 2.9 fusion.181
  43.6 4.2 collective-permute-start.5
  49.2 3.6 collective-permute-start.6
  52.9 2.3 collective-permute-done.7
  57.2 3.4 collective-permute-start.9
  62.0 3.9 collective-permute-start.10
  68.0 133.2 %all-reduce.2 = (f32[2]{0:T(128)S(1)}, f32[2]{0:T(128)S(1)}) all-reduce(f32[2]{0:T(128)S(1)} %get-tuple-element.298, f32[2]{0:T(128)S(1)} %get-tuple-element.297), channel_id=1, replica_groups=mesh['member'=2,'gridy'=8,'gridx'=8] {'gridy','gridx'}, use_global_device_ids=true, to_apply=%region_4.5 | all-reduce | flops 4 | bytes 32 | tf_op jit(solution)/shard_map/psum | solution.py:71
  201.4 139.0 %psum.100 = f32[2]{0:T(128)S(1)} all-reduce(f32[2]{0:T(128)S(1)} %get-tuple-element.316), channel_id=1, replica_groups=mesh['member'=2,'gridy'=8,'gridx'=8] {'gridy','gridx'}, use_global_device_ids=true, to_apply=%region_8.9 | all-reduce | flops 2 | bytes 16 | tf_op jit(solution)/shard_map/psum | solution.py:71
  340.5 11.4 collective-permute-start.13
  354.9 1.8 collective-permute-start.14
  358.8 133.5 %psum.101 = f32[2]{0:T(128)S(1)} all-reduce(f32[2]{0:T(128)S(1)} %get-tuple-element.314), channel_id=1, replica_groups=mesh['member'=2,'gridy'=8,'gridx'=8] {'gridy','gridx'}, use_global_device_ids=true, to_apply=%region_10.11 | all-reduce | flops 2 | bytes 16 | tf_op jit(solution)/shard_map/psum | solution.py:85
  492.5 139.0 %psum.102 = f32[2]{0:T(128)S(1)} all-reduce(f32[2]{0:T(128)S(1)} %multiply_reduce_fusion.5), channel_id=1, replica_groups=mesh['member'=2,'gridy'=8,'gridx'=8] {'gridy','gridx'}, use_global_device_ids=true, to_apply=%region_12.13 | all-reduce | flops 2 | bytes 16 | tf_op jit(solution)/shard_map/psum | solution.py:71
  632.1 11.4 collective-permute-start.17
  644.8 1.9 collective-permute-start.19
  651.0 3.5 bitcast_dynamic-update-slice_fusion.3
  654.5 134.3 %psum.103 = f32[2]{0:T(128)} all-reduce(f32[2]{0:T(128)} %fusion.143), channel_id=1, replica_groups=mesh['member'=2,'gridy'=8,'gridx'=8] {'gridy','gridx'}, use_global_device_ids=true, to_apply=%region_14.15 | all-reduce | flops 2 | bytes 16 | tf_op jit(solution)/shard_map/psum | solution.py:85
  790.5 11.7 collective-permute-start.21
  802.2 3.5 bitcast_dynamic-update-slice_fusion.2
  805.9 3.6 collective-permute-start.22
  816.5 4.1 collective-permute-start.25
  822.3 2.1 fusion.185
  824.4 2.5 copy.20
  826.9 2.5 copy.18
  829.4 3.9 collective-permute-start.26
  833.2 3.0 pad_maximum_fusion.3
  837.5 2.2 scatter-mul.101
  839.7 2.2 scatter-mul.100
  841.9 2.4 copy.21
  844.3 2.5 copy.19
  846.8 3.4 fusion.175
  850.3 3.0 fusion.173
  853.3 3.7 collective-permute-start.29
  859.0 3.6 collective-permute-start.30
  867.7 3.6 collective-permute-start.33
  873.2 3.6 collective-permute-start.34
  881.4 1.8 multiply_reduce_fusion.3
  883.2 131.9 %all-reduce.1 = (f32[2]{0:T(128)}, f32[2]{0:T(128)}) all-reduce(f32[2]{0:T(128)} %get-tuple-element.296, f32[2]{0:T(128)} %get-tuple-element.295), channel_id=1, replica_groups=mesh['member'=2,'gridy'=8,'gridx'=8] {'gridy','gridx'}, use_global_device_ids=true, to_apply=%region_19.20 | all-reduce | flops 4 | bytes 32 | tf_op jit(solution)/shard_map/psum | solution.py:71
  1017.1 140.1 %psum.106 = f32[2]{0:T(128)S(1)} all-reduce(f32[2]{0:T(128)} %get-tuple-element.307), channel_id=1, replica_groups=mesh['member'=2,'gridy'=8,'gridx'=8] {'gridy','gridx'}, use_global_device_ids=true, to_apply=%region_23.24 | all-reduce | flops 2 | bytes 16 | tf_op jit(solution)/shard_map/psum | solution.py:71
  1158.9 11.7 collective-permute-start.37
  1172.7 3.4 collective-permute-start.38
  1180.7 2.4 multiply_reduce_fusion.1
  1183.0 131.7 %psum.107 = f32[2]{0:T(128)} all-reduce(f32[2]{0:T(128)} %get-tuple-element.305), channel_id=1, replica_groups=mesh['member'=2,'gridy'=8,'gridx'=8] {'gridy','gridx'}, use_global_device_ids=true, to_apply=%region_25.26 | all-reduce | flops 2 | bytes 16 | tf_op jit(solution)/shard_map/psum | solution.py:85
  1317.6 141.2 %psum.108 = f32[2]{0:T(128)} all-reduce(f32[2]{0:T(128)} %multiply_reduce_fusion), channel_id=1, replica_groups=mesh['member'=2,'gridy'=8,'gridx'=8] {'gridy','gridx'}, use_global_device_ids=true, to_apply=%region_27.28 | all-reduce | flops 2 | bytes 16 | tf_op jit(solution)/shard_map/psum | solution.py:71
  1460.6 11.8 collective-permute-start.41
  1474.3 3.6 collective-permute-start.42
  1482.5 2.0 fusion.107
  1484.5 131.7 %psum.109 = f32[2]{0:T(128)} all-reduce(f32[2]{0:T(128)} %fusion.107), channel_id=1, replica_groups=mesh['member'=2,'gridy'=8,'gridx'=8] {'gridy','gridx'}, use_global_device_ids=true, to_apply=%region_29.30 | all-reduce | flops 2 | bytes 16 | tf_op jit(solution)/shard_map/psum | solution.py:85
  1617.8 11.5 collective-permute-start.45
  1639.8 3.4 fusion.87
  1643.2 1.9 fusion.50
  1648.0 16.1 psum.110
  1664.8 9.2 all_gather.10
  1674.0 21.4 %psum.111 = f32[2]{0:T(128)S(1)} all-reduce(f32[2]{0:T(128)S(1)} %broadcast_multiply_fusion.9), channel_id=1, replica_groups=mesh['member'=2,'gridy'=8,'gridx'=8] {'gridy'}, use_global_device_ids=true, to_apply=%region_34.35 | all-reduce | flops 2 | bytes 16 | tf_op jit(solution)/shard_map/psum | solution.py:156
  1696.2 5.8 all-reduce
  1705.1 7.6 all-gather.2.cloned.1.call-done
  1712.7 2.9 gather_fusion
  (325 shorter events, 98.7 us)
Async XLA Ops:
  7.2 1705.5 %all-gather.2.cloned.1.call-start = ((), (), s32[]{:S(2)}) async-start(), calls=%async_computation | async-start | bytes 6291456 | tf_op jit(solution)/shard_map/all_gather | solution.py:159
  11.0 29.6 %copy-start = (f32[5,2,4,64,256]{4,3,2,1,0:T(8,128)}, f32[5,2,4,64,256]{4,3,2,1,0:T(8,128)S(1)}, u32[]{:S(2)}) copy-start(f32[5,2,4,64,256]{4,3,2,1,0:T(8,128)S(1)} %constant_dynamic-update-slice_fusion) | copy-start | bytes 7864324
  11.0 4.3 collective-permute-start.1
  12.5 3.0 collective-permute-start
  14.2 23.4 %copy-start.44 = (f32[64]{0:T(128)}, f32[64]{0:T(128)S(1)}, u32[]{:S(2)}) copy-start(f32[64]{0:T(128)S(1)} %get-tuple-element.412) | copy-start | bytes 772
  19.9 14.3 collective-permute-start.3
  23.1 12.8 collective-permute-start.2
  43.6 11.7 copy-start.25
  43.6 5.0 collective-permute-start.5
  47.8 1.2 collective-permute-start.4
  49.1 6.2 collective-permute-start.7
  49.2 6.9 collective-permute-start.6
  57.2 4.2 collective-permute-start.9
  60.6 1.2 collective-permute-start.8
  61.9 5.7 collective-permute-start.11
  62.0 5.7 collective-permute-start.10
  201.2 139.2 %copy-start.47 = (f32[2]{0:T(128)}, f32[2]{0:T(128)S(1)}, u32[]{:S(2)}) copy-start(f32[2]{0:T(128)S(1)} %div.41) | copy-start | bytes 28
  340.5 12.2 collective-permute-start.13
  351.9 1.2 collective-permute-start.12
  353.1 5.4 collective-permute-start.15
  354.9 3.6 collective-permute-start.14
  492.3 152.5 %copy-start.42 = (f32[2]{0:T(128)}, f32[2]{0:T(128)S(1)}, u32[]{:S(2)}) copy-start(f32[2]{0:T(128)S(1)} %div.43) | copy-start | bytes 28
  632.1 18.1 %copy-start.12 = (f32[2,64,256]{2,1,0:T(8,128)}, f32[2,64,256]{2,1,0:T(8,128)S(1)}, u32[]{:S(2)}) copy-start(f32[2,64,256]{2,1,0:T(8,128)S(1)} %multiply_add_fusion.4) | copy-start | bytes 393220
  632.1 12.2 collective-permute-start.17
  643.5 1.2 collective-permute-start.16
  644.8 5.4 collective-permute-start.19
  646.7 3.5 collective-permute-start.18
  790.4 20.8 %copy-start.26 = (f32[2,64,256]{2,1,0:T(8,128)}, f32[2,64,256]{2,1,0:T(8,128)S(1)}, u32[]{:S(2)}) copy-start(f32[2,64,256]{2,1,0:T(8,128)S(1)} %multiply_add_fusion.3) | copy-start | bytes 393220
  790.4 15.3 collective-permute-start.20
  790.5 15.2 collective-permute-start.21
  805.8 5.4 collective-permute-start.23
  805.9 5.3 collective-permute-start.22
  811.9 38.3 %copy-start.16 = (f32[2,64,256]{2,1,0:T(8,128)}, f32[2,64,256]{2,1,0:T(8,128)S(1)}, u32[]{:S(2)}) copy-start(f32[2,64,256]{2,1,0:T(8,128)S(1)} %get-tuple-element.377) | copy-start | bytes 393220
  815.1 35.2 %copy-start.14 = (f32[2,64,256]{2,1,0:T(8,128)}, f32[2,64,256]{2,1,0:T(8,128)S(1)}, u32[]{:S(2)}) copy-start(f32[2,64,256]{2,1,0:T(8,128)S(1)} %subtract_multiply_fusion.4) | copy-start | bytes 393220
  816.5 5.0 collective-permute-start.25
  820.6 1.2 collective-permute-start.24
  826.9 15.0 collective-permute-start.27
  829.4 14.9 collective-permute-start.26
  850.2 12.3 copy-start.23
  853.3 10.2 copy-start.24
  853.3 4.6 collective-permute-start.29
  857.0 1.2 collective-permute-start.28
  859.0 7.2 collective-permute-start.31
  859.0 7.3 collective-permute-start.30
  867.7 4.5 collective-permute-start.33
  871.3 1.2 collective-permute-start.32
  873.2 7.6 collective-permute-start.35
  873.2 8.2 collective-permute-start.34
  1158.9 12.5 collective-permute-start.37
  1170.6 1.2 collective-permute-start.36
  1172.5 8.1 collective-permute-start.39
  1172.7 8.0 collective-permute-start.38
  1460.6 18.4 %copy-start.13 = (f32[2,64,256]{2,1,0:T(8,128)}, f32[2,64,256]{2,1,0:T(8,128)S(1)}, u32[]{:S(2)}) copy-start(f32[2,64,256]{2,1,0:T(8,128)S(1)} %multiply_add_fusion.1) | copy-start | bytes 393220
  1460.6 12.6 collective-permute-start.41
  1472.4 1.2 collective-permute-start.40
  1473.2 6.5 copy-start.37
  1474.3 8.2 collective-permute-start.43
  1474.3 8.2 collective-permute-start.42
  1617.8 18.1 %copy-start.27 = (f32[2,64,256]{2,1,0:T(8,128)}, f32[2,64,256]{2,1,0:T(8,128)S(1)}, u32[]{:S(2)}) copy-start(f32[2,64,256]{2,1,0:T(8,128)S(1)} %multiply_add_fusion) | copy-start | bytes 393220
  1617.8 12.3 collective-permute-start.45
  1629.3 1.2 collective-permute-start.44
  1630.6 5.4 collective-permute-start.47
  1632.4 3.6 collective-permute-start.46
  1645.2 19.6 %copy-start.28 = (f32[2,64,256]{2,1,0:T(8,128)S(1)}, f32[2,64,256]{2,1,0:T(8,128)}, u32[]{:S(2)}) copy-start(f32[2,64,256]{2,1,0:T(8,128)} %copy-done.27) | copy-start | bytes 393220
  (38 other events, 119.4 us)
Sparse Core Ops, SparseCore 0:
  1646.8 65.7 all-gather.1
where the time goes:
time: 1730 us; the launch traced here: 1720 us
  blocking collectives  1410 us (82%)
  starting transfers between devices  137 us (8%)
  other arithmetic  72.2 us (4%)
  local copies, waits for them, and re-layouts  59.9 us (3%)
  waiting for transfers between devices  31 us (2%)
    psum x6, blocking collectives, squared_norm(): return lax.psum(member_total(residual * residual), ('gridy', 'gridx'))  825 us
    psum x4, blocking collectives, surface_solve(): lax.psum(member_total(direction * image), ('gridy', 'gridx'))  531 us
    ppermute x24, starting transfers between devices, padded_2(): lax.ppermute(lax.slice_in_dim(block, 0, width, axis=dim), axis, backward)  128 us
  transfers between devices with their start and end apart: 49, of which 31 were waited for; matrix products, arithmetic and copies ran while one was open for 3% of the time, Pallas kernels for 0%

commit v1 on v0

--- a/solution.py
+++ b/solution.py
@@ -68,7 +68,7 @@
 
 
 def squared_norm(residual):
-    return lax.psum(member_total(residual * residual), ("gridy", "gridx"))
+    return lax.psum(lax.psum(member_total(residual * residual), "gridx"), "gridy")
 
 
 def widen(values):

time: 1730 us -> 1350 us (0.78)
  blocking collectives: 1410 us -> 1070 us
  starting transfers between devices: 137 us -> 97.4 us
    psum x6 -> x12, blocking collectives: 825 us -> 237 us  [the longest x6 151 us: squared_norm(): lax.psum(lax.psum(member_total(residual * residual), 'gridx'), 'gridy')]
    psum x4 -> x6, blocking collectives: 531 us -> 780 us  [surface_solve(): lax.psum(member_total(direction * image), ('gridy', 'gridx'))]
    ppermute x24, starting transfers between devices: 128 us -> 86.6 us  [padded_2(): lax.ppermute(lax.slice_in_dim(block, 0, width, axis=dim), axis, backward)]
  transfers between devices with their start and end apart: 49 -> 49, of which waited for: 31 -> 29; matrix products, arithmetic and copies ran while one was open for 3% -> 4% of each run, Pallas kernels for 0% -> 0%
where the time goes in v1:
time: 1350 us
  blocking collectives  1070 us (79%)
  starting transfers between devices  97.4 us (7%)
  other arithmetic  72.3 us (5%)
  local copies, waits for them, and re-layouts  60.1 us (4%)
  waiting for transfers between devices  31.9 us (2%)
  between operations  16.3 us (1%)
    psum x6, blocking collectives, surface_solve(): lax.psum(member_total(direction * image), ('gridy', 'gridx'))  780 us
    psum x6, blocking collectives, squared_norm(): lax.psum(lax.psum(member_total(residual * residual), 'gridx'), 'gridy')  151 us
    ppermute x24, starting transfers between devices, padded_2(): lax.ppermute(lax.slice_in_dim(block, 0, width, axis=dim), axis, backward)  86.6 us
    psum x6, blocking collectives, squared_norm(): lax.psum(member_total(residual * residual), 'gridx')  86.5 us
  transfers between devices with their start and end apart: 49, of which 29 were waited for; matrix products, arithmetic and copies ran while one was open for 4% of the time, Pallas kernels for 0%

profile of v1, /device:TPU:1, one launch (start us, length us, event | category | flops | bytes accessed | tf_op | source)
XLA Modules:
  0.0 1347.6 jit_solution(5584272420258410526)
XLA Ops:
  15.9 2.1 fusion.186
  23.1 3.5 collective-permute-start.2
  26.7 3.0 pad_maximum_fusion.5
  29.8 2.2 scatter-mul.81
  32.0 2.2 scatter-mul.80
  37.7 2.9 fusion.179
  40.8 2.9 fusion.181
  43.7 4.2 collective-permute-start.5
  49.3 3.6 collective-permute-start.6
  53.0 2.3 collective-permute-done.7
  57.3 3.4 collective-permute-start.9
  62.1 3.9 collective-permute-start.10
  68.1 16.6 %psum.140 = f32[2]{0:T(128)S(1)} all-reduce(f32[2]{0:T(128)S(1)} %get-tuple-element.298), channel_id=1, replica_groups=mesh['member'=2,'gridy'=8,'gridx'=8] {'gridx'}, use_global_device_ids=true, to_apply=%region_4.5 | all-reduce | flops 2 | bytes 16 | tf_op jit(solution)/shard_map/psum | solution.py:71
  84.7 19.5 %psum.141 = f32[2]{0:T(128)S(1)} all-reduce(f32[2]{0:T(128)S(1)} %psum.140), channel_id=1, replica_groups=mesh['member'=2,'gridy'=8,'gridx'=8] {'gridy'}, use_global_device_ids=true, to_apply=%region_5.6 | all-reduce | flops 2 | bytes 16 | tf_op jit(solution)/shard_map/psum | solution.py:71
  104.2 127.4 %psum.142 = f32[2]{0:T(128)S(1)} all-reduce(f32[2]{0:T(128)S(1)} %get-tuple-element.297), channel_id=1, replica_groups=mesh['member'=2,'gridy'=8,'gridx'=8] {'gridy','gridx'}, use_global_device_ids=true, to_apply=%region_7.8 | all-reduce | flops 2 | bytes 16 | tf_op jit(solution)/shard_map/psum | solution.py:85
  231.7 14.0 %psum.143 = f32[2]{0:T(128)S(1)} all-reduce(f32[2]{0:T(128)S(1)} %get-tuple-element.312), channel_id=1, replica_groups=mesh['member'=2,'gridy'=8,'gridx'=8] {'gridx'}, use_global_device_ids=true, to_apply=%region_9.10 | all-reduce | flops 2 | bytes 16 | tf_op jit(solution)/shard_map/psum | solution.py:71
  245.8 27.8 %psum.144 = f32[2]{0:T(128)S(1)} all-reduce(f32[2]{0:T(128)S(1)} %psum.143), channel_id=1, replica_groups=mesh['member'=2,'gridy'=8,'gridx'=8] {'gridy'}, use_global_device_ids=true, to_apply=%region_10.11 | all-reduce | flops 2 | bytes 16 | tf_op jit(solution)/shard_map/psum | solution.py:71
  276.9 3.6 collective-permute-start.14
  282.4 132.0 %psum.145 = f32[2]{0:T(128)S(1)} all-reduce(f32[2]{0:T(128)S(1)} %get-tuple-element.310), channel_id=1, replica_groups=mesh['member'=2,'gridy'=8,'gridx'=8] {'gridy','gridx'}, use_global_device_ids=true, to_apply=%region_12.13 | all-reduce | flops 2 | bytes 16 | tf_op jit(solution)/shard_map/psum | solution.py:85
  414.6 12.8 psum.146
  427.5 26.9 %psum.147 = f32[2]{0:T(128)S(1)} all-reduce(f32[2]{0:T(128)S(1)} %psum.146), channel_id=1, replica_groups=mesh['member'=2,'gridy'=8,'gridx'=8] {'gridy'}, use_global_device_ids=true, to_apply=%region_15.16 | all-reduce | flops 2 | bytes 16 | tf_op jit(solution)/shard_map/psum | solution.py:71
  459.6 2.2 collective-permute-start.18
  464.4 3.5 bitcast_dynamic-update-slice_fusion.3
  467.9 132.4 %psum.148 = f32[2]{0:T(128)} all-reduce(f32[2]{0:T(128)} %fusion.143), channel_id=1, replica_groups=mesh['member'=2,'gridy'=8,'gridx'=8] {'gridy','gridx'}, use_global_device_ids=true, to_apply=%region_17.18 | all-reduce | flops 2 | bytes 16 | tf_op jit(solution)/shard_map/psum | solution.py:85
  602.1 11.7 collective-permute-start.21
  613.8 3.5 bitcast_dynamic-update-slice_fusion.2
  617.5 3.6 collective-permute-start.22
  628.3 4.0 collective-permute-start.25
  633.9 2.1 fusion.185
  636.0 2.5 copy.20
  638.5 2.5 copy.18
  641.0 3.9 collective-permute-start.26
  644.8 3.0 pad_maximum_fusion.3
  649.1 2.2 scatter-mul.101
  651.3 2.2 scatter-mul.100
  653.5 2.4 copy.21
  655.9 2.5 copy.19
  658.4 3.4 fusion.175
  661.8 3.0 fusion.173
  664.9 3.7 collective-permute-start.29
  670.6 3.6 collective-permute-start.30
  679.2 3.7 collective-permute-start.33
  684.8 3.6 collective-permute-start.34
  694.8 14.8 %psum.149 = f32[2]{0:T(128)} all-reduce(f32[2]{0:T(128)} %get-tuple-element.296), channel_id=1, replica_groups=mesh['member'=2,'gridy'=8,'gridx'=8] {'gridx'}, use_global_device_ids=true, to_apply=%region_22.23 | all-reduce | flops 2 | bytes 16 | tf_op jit(solution)/shard_map/psum | solution.py:71
  709.6 20.1 %psum.150 = f32[2]{0:T(128)} all-reduce(f32[2]{0:T(128)} %psum.149), channel_id=1, replica_groups=mesh['member'=2,'gridy'=8,'gridx'=8] {'gridy'}, use_global_device_ids=true, to_apply=%region_23.24 | all-reduce | flops 2 | bytes 16 | tf_op jit(solution)/shard_map/psum | solution.py:71
  729.7 128.0 %psum.151 = f32[2]{0:T(128)} all-reduce(f32[2]{0:T(128)} %get-tuple-element.295), channel_id=1, replica_groups=mesh['member'=2,'gridy'=8,'gridx'=8] {'gridy','gridx'}, use_global_device_ids=true, to_apply=%region_25.26 | all-reduce | flops 2 | bytes 16 | tf_op jit(solution)/shard_map/psum | solution.py:85
  859.6 14.1 %psum.152 = f32[2]{0:T(128)S(1)} all-reduce(f32[2]{0:T(128)} %get-tuple-element.303), channel_id=1, replica_groups=mesh['member'=2,'gridy'=8,'gridx'=8] {'gridx'}, use_global_device_ids=true, to_apply=%region_27.28 | all-reduce | flops 2 | bytes 16 | tf_op jit(solution)/shard_map/psum | solution.py:71
  873.7 27.9 %psum.153 = f32[2]{0:T(128)S(1)} all-reduce(f32[2]{0:T(128)S(1)} %psum.152), channel_id=1, replica_groups=mesh['member'=2,'gridy'=8,'gridx'=8] {'gridy'}, use_global_device_ids=true, to_apply=%region_28.29 | all-reduce | flops 2 | bytes 16 | tf_op jit(solution)/shard_map/psum | solution.py:71
  907.0 3.6 collective-permute-start.38
  915.2 2.4 multiply_reduce_fusion.1
  917.6 130.0 %psum.154 = f32[2]{0:T(128)} all-reduce(f32[2]{0:T(128)} %get-tuple-element.301), channel_id=1, replica_groups=mesh['member'=2,'gridy'=8,'gridx'=8] {'gridy','gridx'}, use_global_device_ids=true, to_apply=%region_30.31 | all-reduce | flops 2 | bytes 16 | tf_op jit(solution)/shard_map/psum | solution.py:85
  1050.4 14.2 %psum.155 = f32[2]{0:T(128)} all-reduce(f32[2]{0:T(128)} %multiply_reduce_fusion), channel_id=1, replica_groups=mesh['member'=2,'gridy'=8,'gridx'=8] {'gridx'}, use_global_device_ids=true, to_apply=%region_32.33 | all-reduce | flops 2 | bytes 16 | tf_op jit(solution)/shard_map/psum | solution.py:71
  1064.6 28.7 %psum.156 = f32[2]{0:T(128)} all-reduce(f32[2]{0:T(128)} %psum.155), channel_id=1, replica_groups=mesh['member'=2,'gridy'=8,'gridx'=8] {'gridy'}, use_global_device_ids=true, to_apply=%region_33.34 | all-reduce | flops 2 | bytes 16 | tf_op jit(solution)/shard_map/psum | solution.py:71
  1098.9 3.6 collective-permute-start.42
  1107.0 2.0 fusion.107
  1109.0 130.0 %psum.157 = f32[2]{0:T(128)} all-reduce(f32[2]{0:T(128)} %fusion.107), channel_id=1, replica_groups=mesh['member'=2,'gridy'=8,'gridx'=8] {'gridy','gridx'}, use_global_device_ids=true, to_apply=%region_35.36 | all-reduce | flops 2 | bytes 16 | tf_op jit(solution)/shard_map/psum | solution.py:85
  1240.7 11.7 collective-permute-start.45
  1263.0 3.4 fusion.87
  1271.2 16.1 %psum.158 = f32[2,4,64]{2,1,0:T(4,128)S(1)} all-reduce(f32[2,4,64]{2,1,0:T(4,128)S(1)} %copy-done.41), channel_id=1, replica_groups=mesh['member'=2,'gridy'=8,'gridx'=8] {'gridx'}, use_global_device_ids=true, to_apply=%region_37.38 | all-reduce | flops 512 | bytes 4096 | tf_op jit(solution)/shard_map/psum | solution.py:154
  1288.0 9.2 all_gather.10
  1297.2 21.4 %psum.159 = f32[2]{0:T(128)S(1)} all-reduce(f32[2]{0:T(128)S(1)} %broadcast_multiply_fusion.9), channel_id=1, replica_groups=mesh['member'=2,'gridy'=8,'gridx'=8] {'gridy'}, use_global_device_ids=true, to_apply=%region_40.41 | all-reduce | flops 2 | bytes 16 | tf_op jit(solution)/shard_map/psum | solution.py:156
  1319.3 5.8 all-reduce
  1328.2 8.0 all-gather.2.cloned.1.call-done
  1336.2 2.9 gather_fusion
  (333 shorter events, 111.7 us)
Async XLA Ops:
  7.2 1329.1 %all-gather.2.cloned.1.call-start = ((), (), s32[]{:S(2)}) async-start(), calls=%async_computation | async-start | bytes 6291456 | tf_op jit(solution)/shard_map/all_gather | solution.py:159
  11.0 29.6 %copy-start = (f32[5,2,4,64,256]{4,3,2,1,0:T(8,128)}, f32[5,2,4,64,256]{4,3,2,1,0:T(8,128)S(1)}, u32[]{:S(2)}) copy-start(f32[5,2,4,64,256]{4,3,2,1,0:T(8,128)S(1)} %constant_dynamic-update-slice_fusion) | copy-start | bytes 7864324
  11.0 4.3 collective-permute-start.1
  12.5 3.0 collective-permute-start
  14.2 23.5 %copy-start.44 = (f32[64]{0:T(128)}, f32[64]{0:T(128)S(1)}, u32[]{:S(2)}) copy-start(f32[64]{0:T(128)S(1)} %get-tuple-element.408) | copy-start | bytes 772
  19.9 14.3 %collective-permute-start.3 = (f32[5,2,4,66,1]{3,2,4,1,0:T(4,128)S(1)}, f32[5,2,4,66,1]{3,2,4,1,0:T(4,128)S(1)}, u32[]{:S(2)}, u32[]{:S(2)}) collective-permute-start(f32[5,2,4,66,1]{3,2,4,1,0:T(4,128)S(1)} %copy.16), channel_id=1, source_target_pairs={{0,1},{1,2},{2,3},{3,4},{4,5},{5,6},{6,7},{7,0},{8,9},{9,10},{10,1... | collective-permute-start | bytes 31688 | tf_op jit(solution)/shard_map/ppermute | solution.py:27
  23.1 12.9 collective-permute-start.2
  43.7 11.7 copy-start.25
  43.7 5.0 collective-permute-start.5
  47.9 1.2 collective-permute-start.4
  49.2 6.2 collective-permute-start.7
  49.3 6.9 collective-permute-start.6
  57.3 4.2 collective-permute-start.9
  60.7 1.2 collective-permute-start.8
  62.0 5.7 collective-permute-start.11
  62.1 5.7 collective-permute-start.10
  231.5 42.0 %copy-start.47 = (f32[2]{0:T(128)}, f32[2]{0:T(128)S(1)}, u32[]{:S(2)}) copy-start(f32[2]{0:T(128)S(1)} %div.41) | copy-start | bytes 28
  273.7 3.0 collective-permute-start.13
  274.3 2.4 collective-permute-start.12
  276.8 5.4 collective-permute-start.15
  276.9 5.3 collective-permute-start.14
  414.4 43.7 %copy-start.42 = (f32[2]{0:T(128)}, f32[2]{0:T(128)S(1)}, u32[]{:S(2)}) copy-start(f32[2]{0:T(128)S(1)} %div.43) | copy-start | bytes 28
  454.9 8.7 copy-start.12
  455.0 3.0 collective-permute-start.17
  455.6 2.4 collective-permute-start.16
  458.1 5.4 collective-permute-start.19
  459.6 4.1 collective-permute-start.18
  602.0 20.9 %copy-start.26 = (f32[2,64,256]{2,1,0:T(8,128)}, f32[2,64,256]{2,1,0:T(8,128)S(1)}, u32[]{:S(2)}) copy-start(f32[2,64,256]{2,1,0:T(8,128)S(1)} %multiply_add_fusion.3) | copy-start | bytes 393220
  602.1 15.2 %collective-permute-start.20 = (f32[1,2,1,256]{3,2,1,0:T(1,128)S(1)}, f32[1,2,1,256]{3,2,1,0:T(1,128)S(1)}, u32[]{:S(2)}, u32[]{:S(2)}) collective-permute-start(f32[1,2,1,256]{3,2,1,0:T(1,128)S(1)} %get-tuple-element.389), channel_id=1, source_target_pairs={{0,8},{8,16},{16,24},{24,32},{32,40},{40,48},{48,56},{56,0},{1,9},... | collective-permute-start | bytes 6152 | tf_op jit(solution)/shard_map/ppermute | solution.py:27
  602.1 15.2 %collective-permute-start.21 = (f32[1,2,1,256]{3,2,1,0:T(1,128)S(1)}, f32[1,2,1,256]{3,2,1,0:T(1,128)S(1)}, u32[]{:S(2)}, u32[]{:S(2)}) collective-permute-start(f32[1,2,1,256]{3,2,1,0:T(1,128)S(1)} %get-tuple-element.390), channel_id=1, source_target_pairs={{8,0},{16,8},{24,16},{32,24},{40,32},{48,40},{56,48},{0,56},{9,1},... | collective-permute-start | bytes 6152 | tf_op jit(solution)/shard_map/ppermute | solution.py:30
  617.4 5.4 collective-permute-start.23
  617.5 5.4 collective-permute-start.22
  623.7 38.1 %copy-start.16 = (f32[2,64,256]{2,1,0:T(8,128)}, f32[2,64,256]{2,1,0:T(8,128)S(1)}, u32[]{:S(2)}) copy-start(f32[2,64,256]{2,1,0:T(8,128)S(1)} %get-tuple-element.373) | copy-start | bytes 393220
  626.8 35.0 %copy-start.14 = (f32[2,64,256]{2,1,0:T(8,128)}, f32[2,64,256]{2,1,0:T(8,128)S(1)}, u32[]{:S(2)}) copy-start(f32[2,64,256]{2,1,0:T(8,128)S(1)} %subtract_multiply_fusion.4) | copy-start | bytes 393220
  628.3 4.8 collective-permute-start.25
  632.2 1.2 collective-permute-start.24
  638.5 15.0 %collective-permute-start.27 = (f32[5,2,4,66,1]{3,2,4,1,0:T(4,128)}, f32[5,2,4,66,1]{3,2,4,1,0:T(4,128)}, u32[]{:S(2)}, u32[]{:S(2)}) collective-permute-start(f32[5,2,4,66,1]{3,2,4,1,0:T(4,128)} %copy.20), channel_id=1, source_target_pairs={{0,1},{1,2},{2,3},{3,4},{4,5},{5,6},{6,7},{7,0},{8,9},{9,10},{10,1... | collective-permute-start | bytes 31688 | tf_op jit(solution)/shard_map/ppermute | solution.py:27
  641.0 14.9 %collective-permute-start.26 = (f32[5,2,4,66,1]{3,2,4,1,0:T(4,128)}, f32[5,2,4,66,1]{3,2,4,1,0:T(4,128)}, u32[]{:S(2)}, u32[]{:S(2)}) collective-permute-start(f32[5,2,4,66,1]{3,2,4,1,0:T(4,128)} %copy.18), channel_id=1, source_target_pairs={{1,0},{2,1},{3,2},{4,3},{5,4},{6,5},{7,6},{0,7},{9,8},{10,9},{11,1... | collective-permute-start | bytes 31688 | tf_op jit(solution)/shard_map/ppermute | solution.py:30
  661.8 12.3 copy-start.23
  664.9 10.2 copy-start.24
  664.9 4.6 collective-permute-start.29
  668.6 1.2 collective-permute-start.28
  670.6 7.3 collective-permute-start.31
  670.6 7.3 collective-permute-start.30
  679.2 4.5 collective-permute-start.33
  682.9 1.2 collective-permute-start.32
  684.8 7.5 collective-permute-start.35
  684.8 8.1 collective-permute-start.34
  903.2 3.0 collective-permute-start.37
  903.9 2.4 collective-permute-start.36
  907.0 8.2 collective-permute-start.39
  907.0 8.2 collective-permute-start.38
  1095.1 8.5 copy-start.13
  1095.1 3.0 collective-permute-start.41
  1095.8 2.4 collective-permute-start.40
  1098.1 6.2 copy-start.37
  1098.9 8.2 collective-permute-start.43
  1098.9 8.2 collective-permute-start.42
  1240.7 18.4 %copy-start.27 = (f32[2,64,256]{2,1,0:T(8,128)}, f32[2,64,256]{2,1,0:T(8,128)S(1)}, u32[]{:S(2)}) copy-start(f32[2,64,256]{2,1,0:T(8,128)S(1)} %multiply_add_fusion) | copy-start | bytes 393220
  1240.7 12.6 collective-permute-start.45
  1252.5 1.2 collective-permute-start.44
  1253.7 5.4 collective-permute-start.47
  1255.7 3.4 collective-permute-start.46
  1268.3 19.6 %copy-start.28 = (f32[2,64,256]{2,1,0:T(8,128)S(1)}, f32[2,64,256]{2,1,0:T(8,128)}, u32[]{:S(2)}) copy-start(f32[2,64,256]{2,1,0:T(8,128)} %copy-done.27) | copy-start | bytes 393220
  (38 other events, 119.0 us)
Sparse Core Ops, SparseCore 0:
  1270.0 66.2 all-gather.1
